TPU v7x, 256 devices: a whole 4x4x8 slice. The times are simulated.
256 devices in a mesh: tm: 16 (over x, y), pairs: 16 (over z, core).
Axes of the slice: x: 4, y: 4, z: 8, core: 2. Of those that a mesh axis runs over, the one named last changes fastest.
Arguments:
- panels: bfloat16 [48, 16, 1024, 128], P('tm', None, 'pairs')
- pair_list: int32 [2, 262144], P(None, ('tm', 'pairs')), may hold values from 0 to 16383, as said below
- pair_count: int32 [256], P(('tm', 'pairs')), may hold values from 1 to 1024, as said below
Outputs:
- stacks: float32 [262144, 512], P(('tm', 'pairs'))
Inputs may be any that keep to these rules, and one draw needn't show every extreme that they name: `pair_list`: slots o * 1024 to (o + 1) * 1024 - 1 belong to owner o. The first channel of each is one of channels o * 64 to (o + 1) * 64 - 1; the second lies 1 to 100 channels after it, in the same section of 1024 channels. A distance of 100 occurs in every draw. Owner o's live slots are its first pair_count[o]. Some owner has all 1024 live in every draw.
All inputs are finite; a program needn't handle non-finite values.
Results may differ from a plain program's by a relative error of at most 0.015.
Values may be sent and summed in bfloat16 or wider, within the bound.
No kernel may reach another device: no remote copies, remote signals or barrier semaphores. Data moves between devices by JAX's collectives and lax.ppermute only.
A program may use at most 128 MiB of HBM per device.

v0:
```python
import math

import jax
import jax.numpy as jnp
import ml_dtypes
import numpy as np
from jax import lax
from jax.experimental import pallas as pl
from jax.experimental.pallas import tpu as pltpu
from jax.sharding import PartitionSpec as P

NB = 100
SEG = 512
SEGS = 12
TILE = 128
QUADS = SEG // TILE
OWN = 64
HALO = 104
REST = HALO - OWN
ROWS = SEGS * 8
PITCH = ROWS + 1
CAP = 1024
UNROLL = 32
LIMIT = 50 << 20
TURNS = 2
BLOCK = 256
VMEM = pl.BlockSpec(memory_space=pltpu.VMEM)
SMEM = pl.BlockSpec(memory_space=pltpu.SMEM)
HBM = pl.BlockSpec(memory_space=pltpu.HBM)


def tables():
    left = np.arange(SEG)[:, None]
    right = np.arange(SEG)[None, :]
    angles = (left * right % (2 * SEG)) * (math.pi / SEG)
    forward = np.concatenate([np.cos(angles), -np.sin(angles)], axis=1) / math.sqrt(SEG)
    angles = (left * (right - SEG // 2) % (2 * SEG)) * (math.pi / SEG)
    weights = np.where(left == 0, 1.0, 2.0) / (math.sqrt(SEG) * SEGS)
    inverse = np.concatenate([weights * np.cos(angles), -weights * np.sin(angles)], axis=0)
    return forward.astype(ml_dtypes.bfloat16), inverse.astype(ml_dtypes.bfloat16)


def aligned(rows):
    return -(-rows // 16) * 16


def spectra(parts, fwd_ref, scaled, loose, spec, first):
    total = sum(part.shape[1] for part in parts)
    pitch = aligned(total)
    for s in range(SEGS):
        base = s * pitch
        for part in parts:
            count = part.shape[1]
            tiles = [part[QUADS * s + q].astype(jnp.float32) for q in range(QUADS)]
            squares = sum(tile * tile for tile in tiles)
            power = jnp.sum(squares, axis=1, keepdims=True) * (1.0 / SEG)
            gain = lax.rsqrt(power + 1e-05)
            for q, tile in enumerate(tiles):
                scaled[pl.ds(base, count), q * TILE:(q + 1) * TILE] = (tile * gain).astype(jnp.bfloat16)
            base += count
    for s in range(0, SEGS, 2):
        rows = scaled[pl.ds(s * pitch, 2 * pitch), :]
        both = jnp.dot(rows, fwd_ref[...], preferred_element_type=jnp.float32)
        for t in range(2):
            for c in range(2 * QUADS):
                half, g = divmod(c, QUADS)
                row = (half * (SEGS // 2) + s // 2) * 8 + t * QUADS + g
                loose[pl.ds(row, total, stride=PITCH), :] = both[
                    t * pitch:t * pitch + total, c * TILE:(c + 1) * TILE]

    def whiten(ch, carry):
        v = [loose[pl.ds(ch * PITCH + r * 8, 8), :] for r in range(SEGS)]
        level = sum(x * x for x in v)
        level = level + pltpu.roll(level, 4, 0)
        gain = lax.rsqrt(level * (1.0 / SEGS) + 0.5)
        for r in range(SEGS):
            spec[pl.ds(pl.multiple_of((first + ch) * ROWS + r * 8, 8), 8), :] = v[r] * gain
        return carry

    lax.fori_loop(0, total, whiten, 0, unroll=4)


def pair_products(count, idx_ref, spec, cross):
    low_half = lax.broadcasted_iota(jnp.int32, (8, TILE), 0) < QUADS

    def step(n, carry):
        for t in range(UNROLL):
            p = n * UNROLL + t
            i = pl.multiple_of(idx_ref[0, p], 8)
            j = pl.multiple_of(idx_ref[1, p], 8)
            real = imag = None
            for h in range(SEGS // 2):
                lr = spec[pl.ds(i + h * 8, 8), :]
                li = spec[pl.ds(i + (SEGS // 2 + h) * 8, 8), :]
                rr = spec[pl.ds(j + h * 8, 8), :]
                ri = spec[pl.ds(j + (SEGS // 2 + h) * 8, 8), :]
                if real is None:
                    real = lr * rr + li * ri
                    imag = li * rr - lr * ri
                else:
                    real = real + lr * rr + li * ri
                    imag = imag + li * rr - lr * ri
            real = real + pltpu.roll(real, QUADS, 0)
            imag = imag + pltpu.roll(imag, QUADS, 0)
            cross[pl.ds(pl.multiple_of(p * 8, 8), 8), :] = jnp.where(low_half, real, imag)
        return carry

    lax.fori_loop(0, (count + UNROLL - 1) // UNROLL, step, 0)


def own_kernel(own_ref, fwd_ref, kept, scaled, loose, spec, sem):
    spectra([own_ref], fwd_ref, scaled, loose, spec, 0)
    copy = pltpu.make_async_copy(spec, kept, sem)
    copy.start()
    copy.wait()


def pair_kernel(idx_ref, live_ref, h1_ref, h2_ref, kept, fwd_ref, inv_ref, out_ref,
                scaled, loose, spec, cross, stacks, sems):
    kept_copy = pltpu.make_async_copy(kept, spec.at[pl.ds(0, OWN * ROWS), :], sems.at[0])
    kept_copy.start()
    spectra([h1_ref, h2_ref], fwd_ref, scaled, loose, spec, OWN)
    kept_copy.wait()
    live = live_ref[0]
    pair_products(live, idx_ref, spec, cross)
    copies = []
    for b in range(CAP // BLOCK):
        rows = pl.ds(b * BLOCK, BLOCK)

        @pl.when(b * BLOCK < live)
        def _():
            columns = [cross[pl.ds(b * BLOCK * 8 + g, BLOCK, stride=8), :].astype(jnp.bfloat16) for g in range(8)]
            lagged = jnp.dot(
                jnp.concatenate(columns, axis=1), inv_ref[...], preferred_element_type=jnp.float32)
            slot = lax.broadcasted_iota(jnp.int32, (BLOCK, SEG), 0) + b * BLOCK
            stacks[rows, :] = jnp.where(slot < live, lagged, 0.0)

        @pl.when(b * BLOCK >= live)
        def _():
            stacks[rows, :] = jnp.zeros((BLOCK, SEG), jnp.float32)

        copies.append(pltpu.make_async_copy(stacks.at[rows, :], out_ref.at[rows, :], sems.at[1 + b]))
        copies[-1].start()
    for copy in copies:
        copy.wait()


def floats(*shape):
    return jax.ShapeDtypeStruct(shape, jnp.float32)


def own_spectra(own, fwd):
    return pl.pallas_call(
        own_kernel,
        out_shape=floats(OWN * ROWS, TILE),
        in_specs=[VMEM, VMEM],
        out_specs=HBM,
        scratch_shapes=[
            pltpu.VMEM((SEGS * OWN, SEG), jnp.bfloat16),
            pltpu.VMEM((OWN * PITCH + 8, TILE), jnp.float32),
            pltpu.VMEM((OWN * ROWS, TILE), jnp.float32),
            pltpu.SemaphoreType.DMA(()),
        ],
        compiler_params=pltpu.CompilerParams(vmem_limit_bytes=LIMIT),
        name="own_spectra",
    )(own, fwd)


def pair_stacks(idx, live, h1, h2, kept, fwd, inv):
    return pl.pallas_call(
        pair_kernel,
        out_shape=floats(CAP, SEG),
        in_specs=[SMEM, SMEM, VMEM, VMEM, HBM, VMEM, VMEM],
        out_specs=HBM,
        scratch_shapes=[
            pltpu.VMEM((SEGS * aligned(HALO), SEG), jnp.bfloat16),
            pltpu.VMEM((HALO * PITCH + 8, TILE), jnp.float32),
            pltpu.VMEM(((OWN + HALO) * ROWS, TILE), jnp.float32),
            pltpu.VMEM((CAP * 8, TILE), jnp.float32),
            pltpu.VMEM((CAP, SEG), jnp.float32),
            pltpu.SemaphoreType.DMA((1 + CAP // BLOCK,)),
        ],
        compiler_params=pltpu.CompilerParams(vmem_limit_bytes=LIMIT),
        name="pair_stacks",
    )(idx, live, h1, h2, kept, fwd, inv)


def turn_kernel(panels, part, whole, held, in_sems, out_sems):
    tiles, sections = panels.shape[:2]
    group = sections // TURNS
    loads, stores = [], []
    for a in range(tiles):
        for n in range(TURNS):
            rows = pl.ds(n * group, group)
            sem = in_sems.at[len(loads)]
            loads.append(pltpu.make_async_copy(panels.at[a, rows], held.at[a, rows], sem))
            loads[-1].start()
    for a in range(tiles):
        for n in range(TURNS):
            rows = pl.ds(n * group, group)
            loads[a * TURNS + n].wait()
            for turned in (whole, part):
                count = turned.shape[2]
                source = held.at[a, rows, pl.ds(0, count), :]
                stores.append(pltpu.make_async_copy(source, turned.at[rows, a], out_sems.at[len(stores)]))
                stores[-1].start()
    for store in stores:
        store.wait()


def turn(panels):
    tiles, sections, _, width = panels.shape
    return pl.pallas_call(
        turn_kernel,
        out_shape=[
            jax.ShapeDtypeStruct((sections, tiles, count, width), panels.dtype) for count in (REST, OWN)],
        in_specs=[HBM],
        out_specs=[HBM] * 2,
        scratch_shapes=[
            pltpu.VMEM(panels.shape, panels.dtype),
            pltpu.SemaphoreType.DMA((tiles * TURNS,)),
            pltpu.SemaphoreType.DMA((2 * tiles * TURNS,)),
        ],
        compiler_params=pltpu.CompilerParams(vmem_limit_bytes=62 << 20),
        name="turn",
    )(panels)


def from_ahead(block, axis, distance):
    devices = range(lax.axis_size(axis))
    route = [(i + distance, i) for i in devices if i + distance in devices]
    return lax.ppermute(block, axis, route)


def by_section(block):
    rows = lax.all_to_all(block, "tm", split_axis=0, concat_axis=0, tiled=True)
    return rows.reshape(-1, *block.shape[2:])


def per_device(panels, pair_list, pair_count):
    fwd, inv = (jnp.asarray(table) for table in tables())
    offset = (lax.axis_index("tm") * lax.axis_size("pairs") + lax.axis_index("pairs")) * OWN
    idx = (pair_list - offset) * ROWS
    part, whole = turn(panels)
    h2_turned = from_ahead(part, "pairs", 2)
    own = by_section(whole)
    h1 = from_ahead(own, "pairs", 1)
    h2 = by_section(h2_turned)
    kept = own_spectra(own, fwd)
    return pair_stacks(idx, pair_count, h1, h2, kept, fwd, inv)


def solution(mesh):
    return jax.shard_map(
        per_device,
        mesh=mesh,
        in_specs=(P("tm", None, "pairs", None), P(None, ("tm", "pairs")), P(("tm", "pairs"))),
        out_specs=P(("tm", "pairs"), None),
        check_vma=False,
    )
```

profile of v0, /device:TPU:96, one launch (start us, length us, event | category | flops | bytes accessed | tf_op | source)
XLA Modules:
  0.0 55.5 jit_solution(5896348850439585819)
XLA Ops:
  0.0 0.0 copy-start
  0.0 0.0 copy-start.2
  0.0 2.2 %turn.1 = (bf16[16,3,40,128]{3,2,1,0:T(8,128)(2,1)}, bf16[16,3,64,128]{3,2,1,0:T(8,128)(2,1)}) custom-call(bf16[3,16,64,128]{3,2,1,0:T(8,128)(2,1)} %panels.1), custom_call_target="tpu_custom_call" | custom-call | tf_op jit(solution)/shard_map/turn/pallas_call | solution.py:213
  2.2 7.0 %all-to-all-start = ((bf16[16,3,64,128]{3,2,1,0:T(8,128)(2,1)}), bf16[16,3,64,128]{3,2,1,0:T(8,128)(2,1)S(1)}, u32[]{:S(2)}, u32[]{:S(2)}) async-start(bf16[16,3,64,128]{3,2,1,0:T(8,128)(2,1)} %get-tuple-element.7), calls=%async_computation | async-start | bytes 1572864 | tf_op jit(solution)/shard_map/all_to_all | solution.py:236
  9.3 2.0 %collective-permute-start.1 = (bf16[16,3,40,128]{3,2,1,0:T(8,128)(2,1)}, bf16[16,3,40,128]{3,2,1,0:T(8,128)(2,1)}, u32[]{:S(2)}, u32[]{:S(2)}) collective-permute-start(bf16[16,3,40,128]{3,2,1,0:T(8,128)(2,1)} %get-tuple-element.8), channel_id=1, source_target_pairs={{2,0},{3,1},{4,2},{5,3},{6,4},{7,5},{8,6},{9,7},{10,8},{11,9},{12,... | collective-permute-start | bytes 1474568 | tf_op jit(solution)/shard_map/ppermute | solution.py:232
  11.3 12.3 %all-to-all-done = bf16[16,3,64,128]{3,2,1,0:T(8,128)(2,1)S(1)} async-done(((bf16[16,3,64,128]{3,2,1,0:T(8,128)(2,1)}), bf16[16,3,64,128]{3,2,1,0:T(8,128)(2,1)S(1)}, u32[]{:S(2)}, u32[]{:S(2)}) %all-to-all-start) | async-done | bytes 786464 | tf_op jit(solution)/shard_map/all_to_all | solution.py:236
  23.6 1.9 %collective-permute-start = (bf16[48,64,128]{2,1,0:T(8,128)(2,1)S(1)}, bf16[48,64,128]{2,1,0:T(8,128)(2,1)S(1)}, u32[]{:S(2)}, u32[]{:S(2)}) collective-permute-start(bf16[48,64,128]{2,1,0:T(8,128)(2,1)S(1)} %bitcast.2), channel_id=1, source_target_pairs={{1,0},{2,1},{3,2},{4,3},{5,4},{6,5},{7,6},{8,7},{9,8},{10,9},{11,1... | collective-permute-start | bytes 2359304 | tf_op jit(solution)/shard_map/ppermute | solution.py:232
  25.6 0.0 collective-permute-done.1
  25.6 6.9 %all-to-all-start.1 = ((bf16[16,3,40,128]{3,2,1,0:T(8,128)(2,1)}), bf16[16,3,40,128]{3,2,1,0:T(8,128)(2,1)S(1)}, u32[]{:S(2)}, u32[]{:S(2)}) async-start(bf16[16,3,40,128]{3,2,1,0:T(8,128)(2,1)} %collective-permute-done.1), calls=%async_computation.1 | async-start | bytes 983040 | tf_op jit(solution)/shard_map/all_to_all | solution.py:236
  33.1 0.0 copy-done.2
  33.2 0.0 copy-done
  33.2 3.4 %own_spectra.1.kept = f32[6144,128]{1,0:T(8,128)} custom-call(bf16[48,64,128]{2,1,0:T(8,128)(2,1)S(1)} %bitcast.3, bf16[512,1024]{1,0:T(8,128)(2,1)S(1)} %copy-done), custom_call_target="tpu_custom_call" | custom-call | tf_op jit(solution)/shard_map/own_spectra/pallas_call | solution.py:153
  36.5 5.9 %all-to-all-done.1 = bf16[16,3,40,128]{3,2,1,0:T(8,128)(2,1)S(1)} async-done(((bf16[16,3,40,128]{3,2,1,0:T(8,128)(2,1)}), bf16[16,3,40,128]{3,2,1,0:T(8,128)(2,1)S(1)}, u32[]{:S(2)}, u32[]{:S(2)}) %all-to-all-start.1) | async-done | bytes 491552 | tf_op jit(solution)/shard_map/all_to_all | solution.py:236
  42.4 0.0 collective-permute-done.h1_ref
  42.4 0.0 copy-start.1
  42.4 1.2 %copy-done.1 = bf16[1024,512]{1,0:T(8,128)(2,1)S(1)} copy-done((bf16[1024,512]{1,0:T(8,128)(2,1)S(1)}, bf16[1024,512]{1,0:T(8,128)(2,1)}, u32[]{:S(2)}) %copy-start.1) | copy-done | bytes 1048600
  43.6 11.8 %pair_stacks.1 = f32[1024,512]{1,0:T(8,128)} custom-call(s32[2,1024]{1,0:T(2,128)S(1)} %subtract_multiply_fusion.idx_ref, s32[1]{0:T(128)S(6)} %copy.6.live_ref, bf16[48,64,128]{2,1,0:T(8,128)(2,1)S(1)} %collective-permute-done.h1_ref, bf16[48,40,128]{2,1,0:T(8,128)(2,1)S(1)} %bitcast.4, f32[6144,128]{1,0:T(8,128)} %own_spectra.1.kept, ...), custom_call_target="tpu_custom_call" | custom-call | tf_op jit(solution)/shard_map/pair_stacks/pallas_call | solution.py:170
  (1 shorter events, 0.0 us)
Async XLA Ops:
  0.0 33.2 %copy-start = (bf16[512,1024]{1,0:T(8,128)(2,1)S(1)}, bf16[512,1024]{1,0:T(8,128)(2,1)}, u32[]{:S(2)}) copy-start(bf16[512,1024]{1,0:T(8,128)(2,1)} %constant.17.clone.fwd_ref) | copy-start | bytes 3145732
  0.0 33.1 %copy-start.2 = (s32[2,1024]{1,0:T(2,128)S(1)}, s32[2,1024]{1,0:T(2,128)}, u32[]{:S(2)}) copy-start(s32[2,1024]{1,0:T(2,128)} %param.6) | copy-start | bytes 24580
  2.2 21.4 %all-to-all-start = ((bf16[16,3,64,128]{3,2,1,0:T(8,128)(2,1)}), bf16[16,3,64,128]{3,2,1,0:T(8,128)(2,1)S(1)}, u32[]{:S(2)}, u32[]{:S(2)}) async-start(bf16[16,3,64,128]{3,2,1,0:T(8,128)(2,1)} %get-tuple-element.7), calls=%async_computation | async-start | bytes 1572864 | tf_op jit(solution)/shard_map/all_to_all | solution.py:236
  9.3 16.3 %collective-permute-start.1 = (bf16[16,3,40,128]{3,2,1,0:T(8,128)(2,1)}, bf16[16,3,40,128]{3,2,1,0:T(8,128)(2,1)}, u32[]{:S(2)}, u32[]{:S(2)}) collective-permute-start(bf16[16,3,40,128]{3,2,1,0:T(8,128)(2,1)} %get-tuple-element.8), channel_id=1, source_target_pairs={{2,0},{3,1},{4,2},{5,3},{6,4},{7,5},{8,6},{9,7},{10,8},{11,9},{12,... | collective-permute-start | bytes 1474568 | tf_op jit(solution)/shard_map/ppermute | solution.py:232
  23.6 18.8 %collective-permute-start = (bf16[48,64,128]{2,1,0:T(8,128)(2,1)S(1)}, bf16[48,64,128]{2,1,0:T(8,128)(2,1)S(1)}, u32[]{:S(2)}, u32[]{:S(2)}) collective-permute-start(bf16[48,64,128]{2,1,0:T(8,128)(2,1)S(1)} %bitcast.2), channel_id=1, source_target_pairs={{1,0},{2,1},{3,2},{4,3},{5,4},{6,5},{7,6},{8,7},{9,8},{10,9},{11,1... | collective-permute-start | bytes 2359304 | tf_op jit(solution)/shard_map/ppermute | solution.py:232
  25.6 16.9 %all-to-all-start.1 = ((bf16[16,3,40,128]{3,2,1,0:T(8,128)(2,1)}), bf16[16,3,40,128]{3,2,1,0:T(8,128)(2,1)S(1)}, u32[]{:S(2)}, u32[]{:S(2)}) async-start(bf16[16,3,40,128]{3,2,1,0:T(8,128)(2,1)} %collective-permute-done.1), calls=%async_computation.1 | async-start | bytes 983040 | tf_op jit(solution)/shard_map/all_to_all | solution.py:236
  42.4 1.2 %copy-start.1 = (bf16[1024,512]{1,0:T(8,128)(2,1)S(1)}, bf16[1024,512]{1,0:T(8,128)(2,1)}, u32[]{:S(2)}) copy-start(bf16[1024,512]{1,0:T(8,128)(2,1)} %constant.18.clone.inv_ref) | copy-start | bytes 3145732
where the time goes:
time: 55.5 us
  waiting for transfers between devices  18.2 us (33%)
  starting transfers between devices  17.9 us (32%)
  Pallas kernels  17.4 us (31%)
  local copies, waits for them, and re-layouts  1.23 us (2%)
  between operations  0.73 us (1%)
    all_to_all x2, waiting for transfers between devices, by_section(): rows = lax.all_to_all(block, 'tm', split_axis=0, concat_axis=0, tiled=True)  18.2 us
    all_to_all x2, starting transfers between devices, by_section(): rows = lax.all_to_all(block, 'tm', split_axis=0, concat_axis=0, tiled=True)  14 us
    pallas_call x1, Pallas kernels, pair_stacks(): pl.pallas_call(pair_kernel, out_shape=floats(CAP, SEG), in_specs=[SMEM, S...  11.8 us
    ppermute x2, starting transfers between devices, from_ahead(): return lax.ppermute(block, axis, route)  3.93 us
    pallas_call x1, Pallas kernels, own_spectra(): pl.pallas_call(own_kernel, out_shape=floats(OWN * ROWS, TILE), in_specs=[...  3.36 us
    pallas_call x1, Pallas kernels, turn(): pl.pallas_call(turn_kernel, out_shape=[jax.ShapeDtypeStruct((sections, ti...  2.21 us
    unnamed x6, local copies, waits for them, and re-layouts  1.23 us
  transfers between devices with their start and end apart: 4, of which 2 were waited for; matrix products, arithmetic and copies ran while one was open for 0% of the time, Pallas kernels for 6%

commit v1 on v0

--- a/solution.py
+++ b/solution.py
@@ -22,6 +22,7 @@
 CAP = 1024
 UNROLL = 32
 LIMIT = 50 << 20
+LAST_LIMIT = 52633 << 10
 TURNS = 2
 BLOCK = 256
 VMEM = pl.BlockSpec(memory_space=pltpu.VMEM)
@@ -115,14 +116,17 @@
     copy.wait()
 
 
-def pair_kernel(idx_ref, live_ref, h1_ref, h2_ref, kept, fwd_ref, inv_ref, out_ref,
-                scaled, loose, spec, cross, stacks, sems):
+def pair_kernel(idx_ref, live_ref, h1_ref, h2_ref, kept, fwd_ref, inv_table, out_ref,
+                scaled, loose, spec, cross, stacks, inv_ref, sems):
     kept_copy = pltpu.make_async_copy(kept, spec.at[pl.ds(0, OWN * ROWS), :], sems.at[0])
     kept_copy.start()
+    inv_copy = pltpu.make_async_copy(inv_table, inv_ref, sems.at[1 + CAP // BLOCK])
+    inv_copy.start()
     spectra([h1_ref, h2_ref], fwd_ref, scaled, loose, spec, OWN)
     kept_copy.wait()
     live = live_ref[0]
     pair_products(live, idx_ref, spec, cross)
+    inv_copy.wait()
     copies = []
     for b in range(CAP // BLOCK):
         rows = pl.ds(b * BLOCK, BLOCK)
@@ -170,7 +174,7 @@
     return pl.pallas_call(
         pair_kernel,
         out_shape=floats(CAP, SEG),
-        in_specs=[SMEM, SMEM, VMEM, VMEM, HBM, VMEM, VMEM],
+        in_specs=[SMEM, SMEM, VMEM, VMEM, HBM, VMEM, HBM],
         out_specs=HBM,
         scratch_shapes=[
             pltpu.VMEM((SEGS * aligned(HALO), SEG), jnp.bfloat16),
@@ -178,9 +182,10 @@
             pltpu.VMEM(((OWN + HALO) * ROWS, TILE), jnp.float32),
             pltpu.VMEM((CAP * 8, TILE), jnp.float32),
             pltpu.VMEM((CAP, SEG), jnp.float32),
-            pltpu.SemaphoreType.DMA((1 + CAP // BLOCK,)),
+            pltpu.VMEM((2 * SEG, SEG), jnp.bfloat16),
+            pltpu.SemaphoreType.DMA((2 + CAP // BLOCK,)),
         ],
-        compiler_params=pltpu.CompilerParams(vmem_limit_bytes=LIMIT),
+        compiler_params=pltpu.CompilerParams(vmem_limit_bytes=LAST_LIMIT),
         name="pair_stacks",
     )(idx, live, h1, h2, kept, fwd, inv)
 

time: 55.5 us -> 54.8 us (0.987)
  local copies, waits for them, and re-layouts: 1.23 us -> 0.01 us
    unnamed x6 -> x4, local copies, waits for them, and re-layouts: 1.23 us -> 0.01 us
where the time goes in v1:
time: 54.8 us
  waiting for transfers between devices  18.2 us (33%)
  Pallas kernels  17.9 us (33%)
  starting transfers between devices  17.9 us (33%)
  between operations  0.73 us (1%)
    all_to_all x2, waiting for transfers between devices, by_section(): rows = lax.all_to_all(block, 'tm', split_axis=0, concat_axis=0, tiled=True)  18.2 us
    all_to_all x2, starting transfers between devices, by_section(): rows = lax.all_to_all(block, 'tm', split_axis=0, concat_axis=0, tiled=True)  14 us
    pallas_call x1, Pallas kernels, pair_stacks(): pl.pallas_call(pair_kernel, out_shape=floats(CAP, SEG), in_specs=[SMEM, S...  12.3 us
    ppermute x2, starting transfers between devices, from_ahead(): return lax.ppermute(block, axis, route)  3.93 us
    pallas_call x1, Pallas kernels, own_spectra(): pl.pallas_call(own_kernel, out_shape=floats(OWN * ROWS, TILE), in_specs=[...  3.35 us
    pallas_call x1, Pallas kernels, turn(): pl.pallas_call(turn_kernel, out_shape=[jax.ShapeDtypeStruct((sections, ti...  2.21 us
  transfers between devices with their start and end apart: 4, of which 2 were waited for; matrix products, arithmetic and copies ran while one was open for 0% of the time, Pallas kernels for 6%

profile of v1, /device:TPU:96, one launch (start us, length us, event | category | flops | bytes accessed | tf_op | source)
XLA Modules:
  0.0 54.8 jit_solution(11293321376015978602)
XLA Ops:
  0.0 0.0 copy-start
  0.0 0.0 copy-start.1
  0.0 2.2 %turn.1 = (bf16[16,3,40,128]{3,2,1,0:T(8,128)(2,1)}, bf16[16,3,64,128]{3,2,1,0:T(8,128)(2,1)}) custom-call(bf16[3,16,64,128]{3,2,1,0:T(8,128)(2,1)} %panels.1), custom_call_target="tpu_custom_call" | custom-call | tf_op jit(solution)/shard_map/turn/pallas_call | solution.py:218
  2.2 7.0 %all-to-all-start = ((bf16[16,3,64,128]{3,2,1,0:T(8,128)(2,1)}), bf16[16,3,64,128]{3,2,1,0:T(8,128)(2,1)S(1)}, u32[]{:S(2)}, u32[]{:S(2)}) async-start(bf16[16,3,64,128]{3,2,1,0:T(8,128)(2,1)} %get-tuple-element.7), calls=%async_computation | async-start | bytes 1572864 | tf_op jit(solution)/shard_map/all_to_all | solution.py:241
  9.3 2.0 %collective-permute-start.1 = (bf16[16,3,40,128]{3,2,1,0:T(8,128)(2,1)}, bf16[16,3,40,128]{3,2,1,0:T(8,128)(2,1)}, u32[]{:S(2)}, u32[]{:S(2)}) collective-permute-start(bf16[16,3,40,128]{3,2,1,0:T(8,128)(2,1)} %get-tuple-element.8), channel_id=1, source_target_pairs={{2,0},{3,1},{4,2},{5,3},{6,4},{7,5},{8,6},{9,7},{10,8},{11,9},{12,... | collective-permute-start | bytes 1474568 | tf_op jit(solution)/shard_map/ppermute | solution.py:237
  11.3 12.3 %all-to-all-done = bf16[16,3,64,128]{3,2,1,0:T(8,128)(2,1)S(1)} async-done(((bf16[16,3,64,128]{3,2,1,0:T(8,128)(2,1)}), bf16[16,3,64,128]{3,2,1,0:T(8,128)(2,1)S(1)}, u32[]{:S(2)}, u32[]{:S(2)}) %all-to-all-start) | async-done | bytes 786464 | tf_op jit(solution)/shard_map/all_to_all | solution.py:241
  23.6 1.9 %collective-permute-start = (bf16[48,64,128]{2,1,0:T(8,128)(2,1)S(1)}, bf16[48,64,128]{2,1,0:T(8,128)(2,1)S(1)}, u32[]{:S(2)}, u32[]{:S(2)}) collective-permute-start(bf16[48,64,128]{2,1,0:T(8,128)(2,1)S(1)} %bitcast.2), channel_id=1, source_target_pairs={{1,0},{2,1},{3,2},{4,3},{5,4},{6,5},{7,6},{8,7},{9,8},{10,9},{11,1... | collective-permute-start | bytes 2359304 | tf_op jit(solution)/shard_map/ppermute | solution.py:237
  25.6 0.0 collective-permute-done.1
  25.6 6.9 %all-to-all-start.1 = ((bf16[16,3,40,128]{3,2,1,0:T(8,128)(2,1)}), bf16[16,3,40,128]{3,2,1,0:T(8,128)(2,1)S(1)}, u32[]{:S(2)}, u32[]{:S(2)}) async-start(bf16[16,3,40,128]{3,2,1,0:T(8,128)(2,1)} %collective-permute-done.1), calls=%async_computation.1 | async-start | bytes 983040 | tf_op jit(solution)/shard_map/all_to_all | solution.py:241
  33.2 0.0 copy-done.1
  33.2 0.0 copy-done
  33.2 3.4 %own_spectra.1.kept = f32[6144,128]{1,0:T(8,128)} custom-call(bf16[48,64,128]{2,1,0:T(8,128)(2,1)S(1)} %bitcast.3, bf16[512,1024]{1,0:T(8,128)(2,1)S(1)} %copy-done), custom_call_target="tpu_custom_call" | custom-call | tf_op jit(solution)/shard_map/own_spectra/pallas_call | solution.py:157
  36.5 5.9 %all-to-all-done.1 = bf16[16,3,40,128]{3,2,1,0:T(8,128)(2,1)S(1)} async-done(((bf16[16,3,40,128]{3,2,1,0:T(8,128)(2,1)}), bf16[16,3,40,128]{3,2,1,0:T(8,128)(2,1)S(1)}, u32[]{:S(2)}, u32[]{:S(2)}) %all-to-all-start.1) | async-done | bytes 491552 | tf_op jit(solution)/shard_map/all_to_all | solution.py:241
  42.4 0.0 collective-permute-done.h1_ref
  42.4 12.3 %pair_stacks.1 = f32[1024,512]{1,0:T(8,128)} custom-call(s32[2,1024]{1,0:T(2,128)S(1)} %subtract_multiply_fusion.idx_ref, s32[1]{0:T(128)S(6)} %copy.6.live_ref, bf16[48,64,128]{2,1,0:T(8,128)(2,1)S(1)} %collective-permute-done.h1_ref, bf16[48,40,128]{2,1,0:T(8,128)(2,1)S(1)} %bitcast.4, f32[6144,128]{1,0:T(8,128)} %own_spectra.1.kept, ...), custom_call_target="tpu_custom_call" | custom-call | tf_op jit(solution)/shard_map/pair_stacks/pallas_call | solution.py:174
  (1 shorter events, 0.0 us)
Async XLA Ops:
  0.0 33.2 %copy-start = (bf16[512,1024]{1,0:T(8,128)(2,1)S(1)}, bf16[512,1024]{1,0:T(8,128)(2,1)}, u32[]{:S(2)}) copy-start(bf16[512,1024]{1,0:T(8,128)(2,1)} %constant.17.clone.fwd_ref) | copy-start | bytes 3145732
  0.0 33.2 %copy-start.1 = (s32[2,1024]{1,0:T(2,128)S(1)}, s32[2,1024]{1,0:T(2,128)}, u32[]{:S(2)}) copy-start(s32[2,1024]{1,0:T(2,128)} %param.6) | copy-start | bytes 24580
  2.2 21.4 %all-to-all-start = ((bf16[16,3,64,128]{3,2,1,0:T(8,128)(2,1)}), bf16[16,3,64,128]{3,2,1,0:T(8,128)(2,1)S(1)}, u32[]{:S(2)}, u32[]{:S(2)}) async-start(bf16[16,3,64,128]{3,2,1,0:T(8,128)(2,1)} %get-tuple-element.7), calls=%async_computation | async-start | bytes 1572864 | tf_op jit(solution)/shard_map/all_to_all | solution.py:241
  9.3 16.3 %collective-permute-start.1 = (bf16[16,3,40,128]{3,2,1,0:T(8,128)(2,1)}, bf16[16,3,40,128]{3,2,1,0:T(8,128)(2,1)}, u32[]{:S(2)}, u32[]{:S(2)}) collective-permute-start(bf16[16,3,40,128]{3,2,1,0:T(8,128)(2,1)} %get-tuple-element.8), channel_id=1, source_target_pairs={{2,0},{3,1},{4,2},{5,3},{6,4},{7,5},{8,6},{9,7},{10,8},{11,9},{12,... | collective-permute-start | bytes 1474568 | tf_op jit(solution)/shard_map/ppermute | solution.py:237
  23.6 18.8 %collective-permute-start = (bf16[48,64,128]{2,1,0:T(8,128)(2,1)S(1)}, bf16[48,64,128]{2,1,0:T(8,128)(2,1)S(1)}, u32[]{:S(2)}, u32[]{:S(2)}) collective-permute-start(bf16[48,64,128]{2,1,0:T(8,128)(2,1)S(1)} %bitcast.2), channel_id=1, source_target_pairs={{1,0},{2,1},{3,2},{4,3},{5,4},{6,5},{7,6},{8,7},{9,8},{10,9},{11,1... | collective-permute-start | bytes 2359304 | tf_op jit(solution)/shard_map/ppermute | solution.py:237
  25.6 16.9 %all-to-all-start.1 = ((bf16[16,3,40,128]{3,2,1,0:T(8,128)(2,1)}), bf16[16,3,40,128]{3,2,1,0:T(8,128)(2,1)S(1)}, u32[]{:S(2)}, u32[]{:S(2)}) async-start(bf16[16,3,40,128]{3,2,1,0:T(8,128)(2,1)} %collective-permute-done.1), calls=%async_computation.1 | async-start | bytes 983040 | tf_op jit(solution)/shard_map/all_to_all | solution.py:241

commit v2 on v1

--- a/solution.py
+++ b/solution.py
@@ -20,7 +20,7 @@
 ROWS = SEGS * 8
 PITCH = ROWS + 1
 CAP = 1024
-UNROLL = 32
+UNROLL = 64
 LIMIT = 50 << 20
 LAST_LIMIT = 52633 << 10
 TURNS = 2

time: 54.8 us -> 55.1 us (level)
  the two profiles are of different devices: /device:TPU:96 before, /device:TPU:64 now
where the time goes in v2:
time: 55.1 us; the launch traced here: 54.9 us
  Pallas kernels  19.3 us (35%)
  waiting for transfers between devices  18.2 us (33%)
  starting transfers between devices  16.7 us (30%)
  between operations  0.74 us (1%)
    all_to_all x2, waiting for transfers between devices, by_section(): rows = lax.all_to_all(block, 'tm', split_axis=0, concat_axis=0, tiled=True)  18.2 us
    pallas_call x1, Pallas kernels, pair_stacks(): pl.pallas_call(pair_kernel, out_shape=floats(CAP, SEG), in_specs=[SMEM, S...  13.7 us
    all_to_all x2, starting transfers between devices, by_section(): rows = lax.all_to_all(block, 'tm', split_axis=0, concat_axis=0, tiled=True)  12.8 us
    ppermute x2, starting transfers between devices, from_ahead(): return lax.ppermute(block, axis, route)  3.93 us
    pallas_call x1, Pallas kernels, own_spectra(): pl.pallas_call(own_kernel, out_shape=floats(OWN * ROWS, TILE), in_specs=[...  3.37 us
    pallas_call x1, Pallas kernels, turn(): pl.pallas_call(turn_kernel, out_shape=[jax.ShapeDtypeStruct((sections, ti...  2.21 us
  transfers between devices with their start and end apart: 4, of which 2 were waited for; matrix products, arithmetic and copies ran while one was open for 0% of the time, Pallas kernels for 6%

profile of v2, /device:TPU:64, one launch (start us, length us, event | category | flops | bytes accessed | tf_op | source)
XLA Modules:
  0.0 54.9 jit_solution(10198172506556029557)
XLA Ops:
  0.0 0.0 copy-start
  0.0 0.0 copy-start.1
  0.0 2.2 %turn.1 = (bf16[16,3,40,128]{3,2,1,0:T(8,128)(2,1)}, bf16[16,3,64,128]{3,2,1,0:T(8,128)(2,1)}) custom-call(bf16[3,16,64,128]{3,2,1,0:T(8,128)(2,1)} %panels.1), custom_call_target="tpu_custom_call" | custom-call | tf_op jit(solution)/shard_map/turn/pallas_call | solution.py:218
  2.2 7.0 %all-to-all-start = ((bf16[16,3,64,128]{3,2,1,0:T(8,128)(2,1)}), bf16[16,3,64,128]{3,2,1,0:T(8,128)(2,1)S(1)}, u32[]{:S(2)}, u32[]{:S(2)}) async-start(bf16[16,3,64,128]{3,2,1,0:T(8,128)(2,1)} %get-tuple-element.7), calls=%async_computation | async-start | bytes 1572864 | tf_op jit(solution)/shard_map/all_to_all | solution.py:241
  9.3 2.0 %collective-permute-start.1 = (bf16[16,3,40,128]{3,2,1,0:T(8,128)(2,1)}, bf16[16,3,40,128]{3,2,1,0:T(8,128)(2,1)}, u32[]{:S(2)}, u32[]{:S(2)}) collective-permute-start(bf16[16,3,40,128]{3,2,1,0:T(8,128)(2,1)} %get-tuple-element.8), channel_id=1, source_target_pairs={{2,0},{3,1},{4,2},{5,3},{6,4},{7,5},{8,6},{9,7},{10,8},{11,9},{12,... | collective-permute-start | bytes 1474568 | tf_op jit(solution)/shard_map/ppermute | solution.py:237
  11.3 12.3 %all-to-all-done = bf16[16,3,64,128]{3,2,1,0:T(8,128)(2,1)S(1)} async-done(((bf16[16,3,64,128]{3,2,1,0:T(8,128)(2,1)}), bf16[16,3,64,128]{3,2,1,0:T(8,128)(2,1)S(1)}, u32[]{:S(2)}, u32[]{:S(2)}) %all-to-all-start) | async-done | bytes 786464 | tf_op jit(solution)/shard_map/all_to_all | solution.py:241
  23.6 1.9 %collective-permute-start = (bf16[48,64,128]{2,1,0:T(8,128)(2,1)S(1)}, bf16[48,64,128]{2,1,0:T(8,128)(2,1)S(1)}, u32[]{:S(2)}, u32[]{:S(2)}) collective-permute-start(bf16[48,64,128]{2,1,0:T(8,128)(2,1)S(1)} %bitcast.2), channel_id=1, source_target_pairs={{1,0},{2,1},{3,2},{4,3},{5,4},{6,5},{7,6},{8,7},{9,8},{10,9},{11,1... | collective-permute-start | bytes 2359304 | tf_op jit(solution)/shard_map/ppermute | solution.py:237
  25.6 0.0 collective-permute-done.1
  25.6 5.7 %all-to-all-start.1 = ((bf16[16,3,40,128]{3,2,1,0:T(8,128)(2,1)}), bf16[16,3,40,128]{3,2,1,0:T(8,128)(2,1)S(1)}, u32[]{:S(2)}, u32[]{:S(2)}) async-start(bf16[16,3,40,128]{3,2,1,0:T(8,128)(2,1)} %collective-permute-done.1), calls=%async_computation.1 | async-start | bytes 983040 | tf_op jit(solution)/shard_map/all_to_all | solution.py:241
  31.9 0.0 copy-done.1
  32.0 0.0 copy-done
  32.0 3.4 %own_spectra.1.kept = f32[6144,128]{1,0:T(8,128)} custom-call(bf16[48,64,128]{2,1,0:T(8,128)(2,1)S(1)} %bitcast.3, bf16[512,1024]{1,0:T(8,128)(2,1)S(1)} %copy-done), custom_call_target="tpu_custom_call" | custom-call | tf_op jit(solution)/shard_map/own_spectra/pallas_call | solution.py:157
  35.4 5.9 %all-to-all-done.1 = bf16[16,3,40,128]{3,2,1,0:T(8,128)(2,1)S(1)} async-done(((bf16[16,3,40,128]{3,2,1,0:T(8,128)(2,1)}), bf16[16,3,40,128]{3,2,1,0:T(8,128)(2,1)S(1)}, u32[]{:S(2)}, u32[]{:S(2)}) %all-to-all-start.1) | async-done | bytes 491552 | tf_op jit(solution)/shard_map/all_to_all | solution.py:241
  41.2 0.0 collective-permute-done.h1_ref
  41.2 13.7 %pair_stacks.1 = f32[1024,512]{1,0:T(8,128)} custom-call(s32[2,1024]{1,0:T(2,128)S(1)} %subtract_multiply_fusion.idx_ref, s32[1]{0:T(128)S(6)} %copy.6.live_ref, bf16[48,64,128]{2,1,0:T(8,128)(2,1)S(1)} %collective-permute-done.h1_ref, bf16[48,40,128]{2,1,0:T(8,128)(2,1)S(1)} %bitcast.4, f32[6144,128]{1,0:T(8,128)} %own_spectra.1.kept, ...), custom_call_target="tpu_custom_call" | custom-call | tf_op jit(solution)/shard_map/pair_stacks/pallas_call | solution.py:174
  (1 shorter events, 0.0 us)
Async XLA Ops:
  0.0 32.0 %copy-start = (bf16[512,1024]{1,0:T(8,128)(2,1)S(1)}, bf16[512,1024]{1,0:T(8,128)(2,1)}, u32[]{:S(2)}) copy-start(bf16[512,1024]{1,0:T(8,128)(2,1)} %constant.17.clone.fwd_ref) | copy-start | bytes 3145732
  0.0 31.9 %copy-start.1 = (s32[2,1024]{1,0:T(2,128)S(1)}, s32[2,1024]{1,0:T(2,128)}, u32[]{:S(2)}) copy-start(s32[2,1024]{1,0:T(2,128)} %param.6) | copy-start | bytes 24580
  2.2 21.4 %all-to-all-start = ((bf16[16,3,64,128]{3,2,1,0:T(8,128)(2,1)}), bf16[16,3,64,128]{3,2,1,0:T(8,128)(2,1)S(1)}, u32[]{:S(2)}, u32[]{:S(2)}) async-start(bf16[16,3,64,128]{3,2,1,0:T(8,128)(2,1)} %get-tuple-element.7), calls=%async_computation | async-start | bytes 1572864 | tf_op jit(solution)/shard_map/all_to_all | solution.py:241
  9.3 16.3 %collective-permute-start.1 = (bf16[16,3,40,128]{3,2,1,0:T(8,128)(2,1)}, bf16[16,3,40,128]{3,2,1,0:T(8,128)(2,1)}, u32[]{:S(2)}, u32[]{:S(2)}) collective-permute-start(bf16[16,3,40,128]{3,2,1,0:T(8,128)(2,1)} %get-tuple-element.8), channel_id=1, source_target_pairs={{2,0},{3,1},{4,2},{5,3},{6,4},{7,5},{8,6},{9,7},{10,8},{11,9},{12,... | collective-permute-start | bytes 1474568 | tf_op jit(solution)/shard_map/ppermute | solution.py:237
  23.6 17.6 %collective-permute-start = (bf16[48,64,128]{2,1,0:T(8,128)(2,1)S(1)}, bf16[48,64,128]{2,1,0:T(8,128)(2,1)S(1)}, u32[]{:S(2)}, u32[]{:S(2)}) collective-permute-start(bf16[48,64,128]{2,1,0:T(8,128)(2,1)S(1)} %bitcast.2), channel_id=1, source_target_pairs={{1,0},{2,1},{3,2},{4,3},{5,4},{6,5},{7,6},{8,7},{9,8},{10,9},{11,1... | collective-permute-start | bytes 2359304 | tf_op jit(solution)/shard_map/ppermute | solution.py:237
  25.6 15.6 %all-to-all-start.1 = ((bf16[16,3,40,128]{3,2,1,0:T(8,128)(2,1)}), bf16[16,3,40,128]{3,2,1,0:T(8,128)(2,1)S(1)}, u32[]{:S(2)}, u32[]{:S(2)}) async-start(bf16[16,3,40,128]{3,2,1,0:T(8,128)(2,1)} %collective-permute-done.1), calls=%async_computation.1 | async-start | bytes 983040 | tf_op jit(solution)/shard_map/all_to_all | solution.py:241
